TPU v7x, 128 devices: a whole 4x4x4 slice. The times are simulated.
128 devices in a mesh: req: 32 (over z, y, x_lo), exp: 4 (over x_hi, core).
Axes of the slice: x: 4 (x_hi: 2, x_lo: 2; x = x_hi * 2 + x_lo), y: 4, z: 4, core: 2. Of those that a mesh axis runs over, the one named last changes fastest.
Arguments:
- hidden_in: bfloat16 [8192, 2048], P(('req', 'exp')), may hold values from -6 to 6
- query_in: bfloat16 [8192, 2048], P('req', 'exp'), may hold values from -6 to 6
- key_in: bfloat16 [8192, 2048], P('req', 'exp'), may hold values from -6 to 6
- value_in: bfloat16 [8192, 2048], P('req', 'exp'), may hold values from -24 to 24
- query_gain: float32 [128], replicated, may hold values from 0.5 to 2.5
- key_gain: float32 [128], replicated, may hold values from 0.5 to 2.5
- cache_keys: bfloat16 [64, 32, 2048], P('req', None, 'exp'), may hold values from -400 to 400
- cache_values: bfloat16 [64, 32, 2048], P('req', None, 'exp'), may hold values from -24 to 24
- cache_block: int32 [128], replicated, may hold values from -1 to 63, as said below
- request_lengths: int32 [32, 4], P('req'), may hold values from 1 to 128, 256 in all within a row
- out_proj: bfloat16 [2048, 2048], P('exp'), may hold values from -0.125 to 0.125
- norm_gain: float32 [2048], replicated, may hold values from 0.25 to 1.75
- expert_ids: int32 [8192, 8], P(('req', 'exp')), may hold values from 0 to 63, all different within a row; in each aligned block of 64 rows (0 to 63, 64 to 127, ...) at most 10 rows name the same one
- gate_values: float32 [8192, 8], P(('req', 'exp')), may hold values from 0.4 to 1.6
- old_slots: int32 [64], replicated, may hold values from 0 to 63, each once
- new_replicas: int32 [32], replicated, may hold values from 0 to 63
- slot_weights: bfloat16 [64, 3, 2048, 1024], P('req', None, None, 'exp'), may hold values from -0.125 to 0.125
Outputs:
- layer_out: bfloat16 [8192, 2048], P(('req', 'exp'))
- replica_weights: bfloat16 [32, 3, 2048, 1024], P('req', None, None, 'exp')
Inputs may be any that keep to these rules, and one draw needn't show every extreme that they name: `cache_block`: each index of req has exactly 2 of its 4 requests with a block; every block serves exactly one request. `expert_ids`: in each aligned block of 64 rows (the rows of one device) no expert is named by more than 10 rows, a bound that some block reaches; the 8 experts of a row differ. `old_slots`: every expert is in exactly one slot. `request_lengths`: the lengths of each index of req sum to 256.
All inputs are finite; a program needn't handle non-finite values.
Results may differ from a plain program's by a relative error of at most 0.025.
Values may be sent and summed in bfloat16 or wider, within the bound.
A program may use at most 128 MiB of HBM per device.

v0:
```python
import math
import jax
import jax.numpy as jnp
from jax import lax
from jax.sharding import PartitionSpec as P


def prepare(values, gain, position):
    vector = values.astype(jnp.float32)
    scaled = vector * lax.rsqrt(jnp.mean(vector * vector, axis=-1, keepdims=True) + 1e-06) * gain
    half_size = scaled.shape[-1] // 2
    frequency = 10000.0 ** (-(jnp.arange(half_size, dtype=jnp.float32) * 2.0 / scaled.shape[-1]))
    angles = position[:, None] * frequency[None, :]
    cosine = jnp.cos(angles)[:, None, :]
    sine_part = jnp.sin(angles)[:, None, :]
    lower_half = scaled[..., :half_size]
    upper_half = scaled[..., half_size:]
    rotated = jnp.concatenate(
        [
            lower_half * cosine - upper_half * sine_part,
            upper_half * cosine + lower_half * sine_part,
        ],
        axis=-1,
    )
    return rotated.astype(jnp.bfloat16)


def compact(block_rows, slots_wanted):
    live = block_rows >= 0
    ranks = jnp.cumsum(live.astype(jnp.int32), axis=1) - 1
    request_idx = jnp.arange(block_rows.shape[1], dtype=jnp.int32)[None, :]
    chosen_blocks = []
    chosen_requests = []
    for slot_num in range(slots_wanted):
        picked = live & (ranks == slot_num)
        chosen_blocks.append(jnp.sum(jnp.where(picked, block_rows, 0), axis=1))
        chosen_requests.append(jnp.sum(jnp.where(picked, request_idx, 0), axis=1))
    return (jnp.stack(chosen_blocks, axis=1), jnp.stack(chosen_requests, axis=1))


def run_slots(inbox, slot_weights, capacity):
    sources = inbox.shape[0]
    model_width = inbox.shape[2]
    slot_count = slot_weights.shape[0]
    grouped = inbox.reshape(sources, slot_count, capacity, model_width)
    results = []
    for slot_num in range(slot_count):
        in_rows = grouped[:, slot_num].reshape(sources * capacity, model_width)
        gate_act = jnp.dot(in_rows, slot_weights[slot_num, 0], preferred_element_type=jnp.float32)
        up_act = jnp.dot(in_rows, slot_weights[slot_num, 1], preferred_element_type=jnp.float32)
        hidden = (jax.nn.silu(gate_act) * up_act).astype(jnp.bfloat16)
        partial_value = lax.dot_general(
            hidden,
            slot_weights[slot_num, 2],
            (((1,), (1,)), ((), ())),
            preferred_element_type=jnp.float32,
        )
        results.append(partial_value.reshape(sources, capacity, model_width))
    return jnp.stack(results, axis=1).reshape(sources, slot_count * capacity, model_width)


def body(
    hidden_in,
    query_in,
    key_in,
    value_in,
    query_gain,
    key_gain,
    cache_keys,
    cache_values,
    cache_block,
    request_lengths,
    out_proj,
    norm_gain,
    expert_ids,
    gate_values,
    old_slots,
    new_replicas,
    slot_weights,
):
    req_count = lax.axis_size("req")
    exp_count = lax.axis_size("exp")
    group_idx = lax.axis_index("req")
    tok_grp, width_q = query_in.shape
    tok_dev, model_width = hidden_in.shape
    head_size = query_gain.shape[0]
    head_count = width_q // head_size
    cache_dev = cache_keys.shape[0]
    pre_len = cache_keys.shape[1]
    req_grp = request_lengths.shape[1]
    lengths = request_lengths[0]
    req_ends = jnp.cumsum(lengths)
    starts = req_ends - lengths
    places = jnp.arange(tok_grp, dtype=jnp.int32)
    member = (places[:, None] >= starts[None, :]) & (places[:, None] < req_ends[None, :])
    request_idx = jnp.arange(req_grp, dtype=jnp.int32)
    segment = jnp.sum(jnp.where(member, request_idx[None, :], 0), axis=1)
    offset = places - jnp.sum(jnp.where(member, starts[None, :], 0), axis=1)
    block_rows = cache_block.reshape(req_count, req_grp)
    my_blocks = lax.dynamic_index_in_dim(block_rows, group_idx, 0, keepdims=False)
    has_cache = my_blocks >= 0
    token_cached = jnp.sum(jnp.where(member & has_cache[None, :], 1, 0), axis=1) > 0
    position = (offset + jnp.where(token_cached, pre_len, 0)).astype(jnp.float32)
    need_blocks, need_requests = compact(block_rows, cache_dev)
    my_requests = lax.dynamic_index_in_dim(need_requests, group_idx, 0, keepdims=False)
    key_width = cache_keys.shape[2]
    rows_per = pre_len // req_count
    both = jnp.concatenate([cache_keys, cache_values], axis=-1)
    both = both.reshape(cache_dev, req_count, rows_per, 2 * key_width).transpose(1, 0, 2, 3)
    spread = lax.all_to_all(both, "req", split_axis=0, concat_axis=0, tiled=True)
    spread = spread.reshape(req_count * cache_dev, rows_per, 2 * key_width)
    picked = jnp.take(spread, need_blocks.reshape(-1), axis=0)
    picked = picked.reshape(req_count, cache_dev, rows_per, 2 * key_width)
    gathered = lax.all_to_all(picked, "req", split_axis=0, concat_axis=0, tiled=True)
    gathered = gathered.transpose(1, 0, 2, 3).reshape(cache_dev, pre_len, 2 * key_width)
    far_keys = gathered[..., :key_width]
    far_values = gathered[..., key_width:]
    query_n = prepare(query_in.reshape(tok_grp, head_count, head_size), query_gain, position)
    key_n = prepare(key_in.reshape(tok_grp, head_count, head_size), key_gain, position)
    keyset = jnp.concatenate(
        [key_n, far_keys.reshape(cache_dev * pre_len, head_count, head_size)], axis=0
    )
    valueset = jnp.concatenate(
        [
            value_in.reshape(tok_grp, head_count, head_size),
            far_values.reshape(cache_dev * pre_len, head_count, head_size),
        ],
        axis=0,
    )
    key_request = jnp.concatenate([segment, jnp.repeat(my_requests, pre_len)])
    allowed = segment[:, None] == key_request[None, :]
    scores = jnp.einsum("qhd,khd->hqk", query_n, keyset, preferred_element_type=jnp.float32) * (
        1.0 / math.sqrt(head_size)
    )
    scores = jnp.where(allowed[None], scores, -1e30)
    peak = jnp.max(scores, axis=-1, keepdims=True)
    expos = jnp.exp(scores - peak)
    weights = (expos / jnp.sum(expos, axis=-1, keepdims=True)).astype(jnp.bfloat16)
    attended = jnp.einsum("hqk,khd->qhd", weights, valueset, preferred_element_type=jnp.float32)
    attended = attended.astype(jnp.bfloat16).reshape(tok_grp, width_q)
    attn_out = lax.psum_scatter(
        jnp.dot(attended, out_proj, preferred_element_type=jnp.float32),
        "exp",
        scatter_dimension=0,
        tiled=True,
    )
    residual = hidden_in.astype(jnp.float32) + attn_out
    normed = (
        residual
        * lax.rsqrt(jnp.mean(residual * residual, axis=-1, keepdims=True) + 1e-06)
        * norm_gain
    ).astype(jnp.bfloat16)
    topk_count = expert_ids.shape[1]
    slot_total = old_slots.shape[0]
    slots_here = slot_weights.shape[0]
    capacity = max(2, tok_dev * topk_count * 5 // (4 * slot_total))
    slot_range = jnp.arange(slot_total, dtype=jnp.int32)
    slot_of = jnp.sum(
        jnp.where(old_slots[None, :] == slot_range[:, None], slot_range[None, :], 0), axis=1
    )
    flat_ids = expert_ids.reshape(-1)
    onehot = flat_ids[:, None] == slot_range[None, :]
    row_slot = jnp.sum(jnp.where(onehot, slot_of[None, :], 0), axis=1)
    before = jnp.cumsum(onehot.astype(jnp.int32), axis=0) - onehot.astype(jnp.int32)
    row_rank = jnp.sum(jnp.where(onehot, before, 0), axis=1)
    target = row_slot * capacity + row_rank
    send_rows = jnp.repeat(normed, topk_count, axis=0)
    outbox = jnp.zeros((slot_total * capacity, model_width), jnp.bfloat16).at[target].set(send_rows)
    outbox = outbox.reshape(req_count, slots_here * capacity, model_width)
    copies = jnp.broadcast_to(
        outbox[:, None], (req_count, exp_count, slots_here * capacity, model_width)
    )
    copies = copies.reshape(req_count * exp_count, slots_here * capacity, model_width)
    inbox = lax.all_to_all(copies, ("req", "exp"), split_axis=0, concat_axis=0, tiled=True)
    partial_value = run_slots(inbox, slot_weights, capacity).astype(jnp.bfloat16)
    returned = lax.all_to_all(
        partial_value, ("req", "exp"), split_axis=0, concat_axis=0, tiled=True
    )
    result = jnp.sum(
        returned.astype(jnp.float32).reshape(
            req_count, exp_count, slots_here * capacity, model_width
        ),
        axis=1,
    )
    result_rows = jnp.take(result.reshape(slot_total * capacity, model_width), target, axis=0)
    mixture = jnp.sum(
        result_rows.reshape(tok_dev, topk_count, model_width) * gate_values[:, :, None], axis=1
    )
    layer_out = (residual + mixture).astype(jnp.bfloat16)
    spread_slots = lax.all_to_all(slot_weights, "req", split_axis=2, concat_axis=0, tiled=True)
    replica_onehot = new_replicas[:, None] == slot_range[None, :]
    source_slot = jnp.sum(jnp.where(replica_onehot, slot_of[None, :], 0), axis=1)
    chosen_pieces = jnp.take(spread_slots, source_slot, axis=0)
    replica_weights = lax.all_to_all(chosen_pieces, "req", split_axis=0, concat_axis=2, tiled=True)
    return (layer_out, replica_weights)


def solution(mesh):
    in_specs = (
        P(("req", "exp"), None),
        P("req", "exp"),
        P("req", "exp"),
        P("req", "exp"),
        P(),
        P(),
        P("req", None, "exp"),
        P("req", None, "exp"),
        P(),
        P("req", None),
        P("exp", None),
        P(),
        P(("req", "exp"), None),
        P(("req", "exp"), None),
        P(),
        P(),
        P("req", None, None, "exp"),
    )
    out_specs = (P(("req", "exp"), None), P("req", None, None, "exp"))
    return jax.shard_map(body, mesh=mesh, in_specs=in_specs, out_specs=out_specs, check_vma=False)
```

profile of v0, /device:TPU:74, one launch (start us, length us, event | category | flops | bytes accessed | tf_op | source)
XLA Modules:
  0.0 696.7 jit_solution(8149768700036297165)
XLA Ops:
  7.2 1.1 copy.100
  8.2 0.9 copy.101
  9.2 0.8 maximum_bitcast_fusion
  9.9 8.5 %all-to-all-start = ((bf16[32,2,1,1024]{3,1,2,0:T(2,128)(2,1)}), bf16[32,2,1,1024]{3,1,2,0:T(2,128)(2,1)S(1)}, u32[]{:S(2)}, u32[]{:S(2)}) async-start(bf16[32,2,1,1024]{3,1,2,0:T(2,128)(2,1)} %maximum_bitcast_fusion), calls=%async_computation | async-start | bytes 262144 | tf_op jit(solution)/shard_map/all_to_all | solution.py:110
  18.5 0.5 negate_power_fusion
  19.0 0.7 reshape.343
  20.8 0.5 compare_bitcast_fusion
  21.6 0.7 reshape.351
  22.3 0.8 reduce-window.10
  23.1 1.2 fusion.52
  24.3 1.1 copy.107
  25.6 1.1 copy.109
  26.9 0.7 select_reduce_fusion.8
  27.7 0.7 pad_add_fusion
  28.4 1.1 multiply_cosine_fusion
  29.5 1.0 multiply_multiply_fusion
  30.5 1.1 subtract_convert_fusion.1
  31.8 1.1 copy.98
  33.1 10.5 %copy.125 = bf16[2,3,2048,256]{3,1,0,2:T(4,128)(2,1)} copy(bf16[2,3,2048,256]{3,2,1,0:T(8,128)(2,1)} %param.33) | data formatting | bytes 12582912 | tf_op args[16]
  43.6 0.7 gather_fusion
  44.4 0.9 broadcast_select_fusion.1
  45.2 8.3 %all-to-all-start.1 = ((bf16[32,2,1,1024]{3,1,2,0:T(2,128)(2,1)}), bf16[32,2,1,1024]{3,1,2,0:T(2,128)(2,1)S(1)}, u32[]{:S(2)}, u32[]{:S(2)}) async-start(bf16[32,2,1,1024]{3,1,2,0:T(2,128)(2,1)} %broadcast_select_fusion.1), calls=%async_computation.1 | async-start | bytes 262144 | tf_op jit(solution)/shard_map/all_to_all | solution.py:114
  53.7 4.9 all-to-all-done.1
  58.6 8.6 %all-to-all-start.4 = ((bf16[2,3,2048,256]{3,1,0,2:T(4,128)(2,1)}), bf16[2,3,2048,256]{3,1,0,2:T(4,128)(2,1)}, u32[]{:S(2)}, u32[]{:S(2)}) async-start(bf16[2,3,2048,256]{3,1,0,2:T(4,128)(2,1)} %copy.125), calls=%async_computation.5 | async-start | bytes 16777216 | tf_op jit(solution)/shard_map/all_to_all | solution.py:190
  67.6 2.7 fusion.67
  70.3 1.7 convolution_convert_fusion
  72.1 2.0 fusion.72
  74.4 1.2 reduce-window.11
  76.2 47.9 %reduce-scatter.2.cloned.1.call-done = f32[64,2048]{1,0:T(8,128)} async-done(((f32[256,2048]{1,0:T(8,128)}), f32[64,2048]{1,0:T(8,128)}) %reduce-scatter.2.cloned.1.call-update) | async-done | bytes 524304 | tf_op jit(solution)/shard_map/reduce_scatter | solution.py:141
  124.1 1.2 multiply_reduce_fusion
  125.3 1.2 multiply_convert_fusion
  126.5 5.5 scatter_custom_fusion
  131.9 5.1 broadcast_in_dim.198
  137.1 37.6 %all-to-all-done.4 = bf16[2,3,2048,256]{3,1,0,2:T(4,128)(2,1)} async-done(((bf16[2,3,2048,256]{3,1,0,2:T(4,128)(2,1)}), bf16[2,3,2048,256]{3,1,0,2:T(4,128)(2,1)}, u32[]{:S(2)}, u32[]{:S(2)}) %all-to-all-start.4) | async-done | bytes 6291488 | tf_op jit(solution)/shard_map/all_to_all | solution.py:190
  174.7 8.1 %broadcast_in_dim.199 = bf16[32,4,20,2048]{3,2,1,0:T(8,128)(2,1)} broadcast(bf16[32,20,2048]{2,1,0:T(8,128)(2,1)} %broadcast_in_dim.198), dimensions={0,2,3} | broadcast | bytes 13107200 | tf_op jit(solution)/shard_map/broadcast_in_dim | solution.py:170
  182.8 20.8 %all-to-all-start.2 = ((bf16[128,20,2048]{2,1,0:T(8,128)(2,1)}), bf16[128,20,2048]{2,1,0:T(8,128)(2,1)}, u32[]{:S(2)}, u32[]{:S(2)}) async-start(bf16[128,20,2048]{2,1,0:T(8,128)(2,1)} %bitcast.121), calls=%async_computation.3 | async-start | bytes 25165824 | tf_op jit(solution)/shard_map/all_to_all | solution.py:174
  203.9 4.9 copy.126
  208.8 3.3 copy.127
  212.1 5.2 gather_fusion.2
  217.3 3.9 broadcast_select_fusion
  221.2 144.9 %all-to-all-done.2 = bf16[128,20,2048]{2,1,0:T(8,128)(2,1)} async-done(((bf16[128,20,2048]{2,1,0:T(8,128)(2,1)}), bf16[128,20,2048]{2,1,0:T(8,128)(2,1)}, u32[]{:S(2)}, u32[]{:S(2)}) %all-to-all-start.2) | async-done | bytes 10485792 | tf_op jit(solution)/shard_map/all_to_all | solution.py:174
  366.2 7.2 %all-to-all-start.5 = ((bf16[32,3,64,256]{3,2,1,0:T(8,128)(2,1)}), bf16[32,3,64,256]{3,2,1,0:T(8,128)(2,1)}, u32[]{:S(2)}, u32[]{:S(2)}) async-start(bf16[32,3,64,256]{3,2,1,0:T(8,128)(2,1)} %broadcast_select_fusion), calls=%async_computation.6 | async-start | bytes 6291456 | tf_op jit(solution)/shard_map/all_to_all | solution.py:194
  373.4 12.7 %copy.116 = bf16[128,20,2048]{2,0,1:T(8,128)(2,1)} copy(bf16[128,20,2048]{2,1,0:T(8,128)(2,1)} %all-to-all-done.2) | data formatting | bytes 20971520 | tf_op jit(solution)/shard_map/all_to_all | solution.py:174
  386.0 10.2 %fusion.65 = (bf16[128,1,10,2048]{3,0,2,1:T(8,128)(2,1)}, bf16[128,1,10,2048]{3,0,2,1:T(8,128)(2,1)}) fusion(bf16[128,2,10,2048]{3,0,2,1:T(8,128)(2,1)} %bitcast.122), kind=kLoop, calls=%fused_computation.134 | loop fusion | bytes 20971520 | tf_op jit(solution)/shard_map/slice | solution.py:48
  396.3 9.0 %copy.117 = bf16[128,1,10,2048]{3,2,0,1:T(8,128)(2,1)} copy(bf16[128,1,10,2048]{3,0,2,1:T(8,128)(2,1)} %get-tuple-element.13) | data formatting | bytes 10485760 | tf_op jit(solution)/shard_map/slice | solution.py:48
  405.3 9.8 %reshape_squeeze.6 = bf16[1280,2048]{1,0:T(8,128)(2,1)} reshape(bf16[128,1,10,2048]{3,2,0,1:T(8,128)(2,1)} %copy.117) | data formatting | bytes 10485760 | tf_op jit(solution)/shard_map/reshape;squeeze | solution.py:48
  415.1 4.5 fusion.17
  419.6 2.9 fusion.3
  422.8 9.0 %copy.119 = bf16[128,1,10,2048]{3,2,0,1:T(8,128)(2,1)} copy(bf16[128,1,10,2048]{3,0,2,1:T(8,128)(2,1)} %get-tuple-element.14) | data formatting | bytes 10485760 | tf_op jit(solution)/shard_map/slice | solution.py:48
  431.8 10.2 %reshape_squeeze.7 = bf16[1280,2048]{1,0:T(8,128)(2,1)} reshape(bf16[128,1,10,2048]{3,2,0,1:T(8,128)(2,1)} %copy.119) | data formatting | bytes 10485760 | tf_op jit(solution)/shard_map/reshape;squeeze | solution.py:48
  442.0 4.5 fusion.14
  446.5 2.9 fusion.4
  449.7 5.0 convert_bitcast_fusion.1
  454.8 5.2 convert_bitcast_fusion
  459.9 9.0 %pad_maximum_fusion = bf16[128,2,10,2048]{3,0,2,1:T(8,128)(2,1)} fusion(bf16[128,1,10,2048]{3,0,2,1:T(8,128)(2,1)} %convert_bitcast_fusion, bf16[128,1,10,2048]{3,0,2,1:T(8,128)(2,1)} %convert_bitcast_fusion.1), kind=kLoop, calls=%fused_computation.6 | loop fusion | flops 5242880 | bytes 20971520 | tf_op jit(solution)/shard_map/stack | solution.py:59
  468.9 14.0 %copy.121 = bf16[128,20,2048]{2,1,0:T(8,128)(2,1)} copy(bf16[128,20,2048]{2,0,1:T(8,128)(2,1)} %bitcast.123) | data formatting | bytes 20971520 | tf_op jit(solution)/shard_map/convert_element_type | solution.py:175
  482.9 10.9 %all-to-all-start.3 = ((bf16[128,20,2048]{2,1,0:T(8,128)(2,1)}), bf16[128,20,2048]{2,1,0:T(8,128)(2,1)}, u32[]{:S(2)}, u32[]{:S(2)}) async-start(bf16[128,20,2048]{2,1,0:T(8,128)(2,1)} %copy.121), calls=%async_computation.4 | async-start | bytes 25165824 | tf_op jit(solution)/shard_map/all_to_all | solution.py:176
  494.0 4.0 copy.128
  498.0 160.7 %all-to-all-done.3 = bf16[128,20,2048]{2,1,0:T(8,128)(2,1)} async-done(((bf16[128,20,2048]{2,1,0:T(8,128)(2,1)}), bf16[128,20,2048]{2,1,0:T(8,128)(2,1)}, u32[]{:S(2)}, u32[]{:S(2)}) %all-to-all-start.3) | async-done | bytes 10485792 | tf_op jit(solution)/shard_map/all_to_all | solution.py:176
  658.8 11.1 %convert_reduce_fusion = f32[32,20,2048]{2,1,0:T(8,128)} fusion(bf16[128,20,2048]{2,1,0:T(8,128)(2,1)} %all-to-all-done.3), kind=kLoop, calls=%fused_computation.5 | loop fusion | flops 9175040 | bytes 15728640 | tf_op jit(solution)/shard_map/reduce_sum | solution.py:179
  669.9 6.8 reshape.362
  676.7 8.1 %gather_fusion.1 = f32[512,2048]{1,0:T(8,128)} fusion(f32[640,2048]{1,0:T(8,128)} %reshape.362, s32[1024]{0:T(1024)S(1)} %pad_clamp_fusion.1), kind=kCustom, calls=%fused_computation.1 | custom fusion | bytes 8390656 | tf_op jit(solution)/shard_map/jit(_take)/gather | solution.py:185
  684.8 4.1 fusion.2
  688.9 0.8 add_convert_fusion
  (86 shorter events, 4.3 us)
Async XLA Ops:
  7.2 64.9 %copy-start = (bf16[512,2048]{1,0:T(8,128)(2,1)S(1)}, bf16[512,2048]{1,0:T(8,128)(2,1)}, u32[]{:S(2)}) copy-start(bf16[512,2048]{1,0:T(8,128)(2,1)} %param.27) | copy-start | bytes 6291460
  9.9 33.6 %all-to-all-start = ((bf16[32,2,1,1024]{3,1,2,0:T(2,128)(2,1)}), bf16[32,2,1,1024]{3,1,2,0:T(2,128)(2,1)S(1)}, u32[]{:S(2)}, u32[]{:S(2)}) async-start(bf16[32,2,1,1024]{3,1,2,0:T(2,128)(2,1)} %maximum_bitcast_fusion), calls=%async_computation | async-start | bytes 262144 | tf_op jit(solution)/shard_map/all_to_all | solution.py:110
  20.1 4.2 copy-start.9
  26.9 4.8 copy-start.10
  33.1 10.5 %copy-start.11 = (s32[64]{0:T(128)S(1)}, s32[64]{0:T(128)}, u32[]{:S(2)}) copy-start(s32[64]{0:T(128)} %fusion.50) | copy-start | bytes 772
  45.2 13.3 %all-to-all-start.1 = ((bf16[32,2,1,1024]{3,1,2,0:T(2,128)(2,1)}), bf16[32,2,1,1024]{3,1,2,0:T(2,128)(2,1)S(1)}, u32[]{:S(2)}, u32[]{:S(2)}) async-start(bf16[32,2,1,1024]{3,1,2,0:T(2,128)(2,1)} %broadcast_select_fusion.1), calls=%async_computation.1 | async-start | bytes 262144 | tf_op jit(solution)/shard_map/all_to_all | solution.py:114
  58.6 116.1 %all-to-all-start.4 = ((bf16[2,3,2048,256]{3,1,0,2:T(4,128)(2,1)}), bf16[2,3,2048,256]{3,1,0,2:T(4,128)(2,1)}, u32[]{:S(2)}, u32[]{:S(2)}) async-start(bf16[2,3,2048,256]{3,1,0,2:T(4,128)(2,1)} %copy.125), calls=%async_computation.5 | async-start | bytes 16777216 | tf_op jit(solution)/shard_map/all_to_all | solution.py:190
  67.2 56.9 %reduce-scatter.2.cloned.1.call-start = ((), (), s32[]{:S(2)}) async-start(), calls=%async_computation.7 | async-start | bytes 2621440 | tf_op jit(solution)/shard_map/reduce_scatter | solution.py:141
  72.0 2.1 copy-start.7
  72.0 3.9 copy-start.12
  72.0 52.1 %copy-start.5 = (bf16[64,2048]{1,0:T(8,128)(2,1)S(1)}, bf16[64,2048]{1,0:T(8,128)(2,1)}, u32[]{:S(2)}) copy-start(bf16[64,2048]{1,0:T(8,128)(2,1)} %param.17) | copy-start | bytes 786436
  72.0 53.3 %copy-start.6 = (f32[2048]{0:T(1024)S(1)}, f32[2048]{0:T(1024)}, u32[]{:S(2)}) copy-start(f32[2048]{0:T(1024)} %param.28) | copy-start | bytes 24580
  182.8 20.9 %copy-start.13 = (s32[32]{0:T(128)S(1)}, s32[32]{0:T(128)}, u32[]{:S(2)}) copy-start(s32[32]{0:T(128)} %param.32) | copy-start | bytes 388
  182.8 183.4 %all-to-all-start.2 = ((bf16[128,20,2048]{2,1,0:T(8,128)(2,1)}), bf16[128,20,2048]{2,1,0:T(8,128)(2,1)}, u32[]{:S(2)}, u32[]{:S(2)}) async-start(bf16[128,20,2048]{2,1,0:T(8,128)(2,1)} %bitcast.121), calls=%async_computation.3 | async-start | bytes 25165824 | tf_op jit(solution)/shard_map/all_to_all | solution.py:174
  366.2 116.8 %all-to-all-start.5 = ((bf16[32,3,64,256]{3,2,1,0:T(8,128)(2,1)}), bf16[32,3,64,256]{3,2,1,0:T(8,128)(2,1)}, u32[]{:S(2)}, u32[]{:S(2)}) async-start(bf16[32,3,64,256]{3,2,1,0:T(8,128)(2,1)} %broadcast_select_fusion), calls=%async_computation.6 | async-start | bytes 6291456 | tf_op jit(solution)/shard_map/all_to_all | solution.py:194
  415.1 4.5 copy-start.2
  442.0 4.5 copy-start.3
  482.9 11.0 %copy-start.8 = (f32[64,8]{0,1:T(8,128)S(1)}, f32[64,8]{0,1:T(8,128)}, u32[]{:S(2)}) copy-start(f32[64,8]{0,1:T(8,128)} %param.30) | copy-start | bytes 6148
  482.9 175.8 %all-to-all-start.3 = ((bf16[128,20,2048]{2,1,0:T(8,128)(2,1)}), bf16[128,20,2048]{2,1,0:T(8,128)(2,1)}, u32[]{:S(2)}, u32[]{:S(2)}) async-start(bf16[128,20,2048]{2,1,0:T(8,128)(2,1)} %copy.121), calls=%async_computation.4 | async-start | bytes 25165824 | tf_op jit(solution)/shard_map/all_to_all | solution.py:176
  676.7 13.0 %copy-start.1 = (bf16[512,2048]{1,0:T(8,128)(2,1)S(1)}, bf16[512,2048]{1,0:T(8,128)(2,1)}, u32[]{:S(2)}) copy-start(bf16[512,2048]{1,0:T(8,128)(2,1)} %param.27) | copy-start | bytes 6291460
  684.8 4.1 copy-start.4
Sparse Core Ops, SparseCore 0:
  74.2 49.7 reduce-scatter.1
where the time goes:
time: 704 us; the launch traced here: 697 us
  waiting for transfers between devices  396 us (56%)
  local copies, waits for them, and re-layouts  146 us (21%)
  starting transfers between devices  64.6 us (9%)
  other arithmetic  43.5 us (6%)
  matrix products  31.5 us (4%)
  between operations  14.8 us (2%)
    all_to_all x1, waiting for transfers between devices, body(): lax.all_to_all(partial_value, ('req', 'exp'), split_axis=0, concat_axis=0...  161 us
    all_to_all x1, waiting for transfers between devices, body(): lax.all_to_all(copies, ('req', 'exp'), split_axis=0, concat_axis=0, tiled...  145 us
    reduce_scatter x1, waiting for transfers between devices, body(): lax.psum_scatter(jnp.dot(attended, out_proj, preferred_element_type=jnp.f...  47.9 us
    all_to_all x1, waiting for transfers between devices, body(): lax.all_to_all(slot_weights, 'req', split_axis=2, concat_axis=0, tiled=True)  37.6 us
    slice x3, local copies, waits for them, and re-layouts, run_slots(): in_rows = grouped[:, slot_num].reshape(sources * capacity, model_width)  28.2 us
    all_to_all x1, starting transfers between devices, body(): lax.all_to_all(copies, ('req', 'exp'), split_axis=0, concat_axis=0, tiled...  20.8 us
    another operation x2, local copies, waits for them, and re-layouts, run_slots(): in_rows = grouped[:, slot_num].reshape(sources * capacity, model_width)  20.1 us
    unnamed x36, local copies, waits for them, and re-layouts  15.9 us
  transfers between devices with their start and end apart: 7, of which 5 were waited for; matrix products, arithmetic and copies ran while one was open for 26% of the time, Pallas kernels for 0%

commit v1 on v0

--- a/solution.py
+++ b/solution.py
@@ -3,6 +3,7 @@
 import jax.numpy as jnp
 from jax import lax
 from jax.sharding import PartitionSpec as P
+from jax.lax import all_to_all, axis_size
 
 
 def prepare(values, gain, position):
@@ -187,7 +188,9 @@
         result_rows.reshape(tok_dev, topk_count, model_width) * gate_values[:, :, None], axis=1
     )
     layer_out = (residual + mixture).astype(jnp.bfloat16)
-    spread_slots = lax.all_to_all(slot_weights, "req", split_axis=2, concat_axis=0, tiled=True)
+    spread_slots = jnp.concatenate(
+        all_to_all(jnp.stack(jnp.split(slot_weights, axis_size("req"), 2), 0), "req", 0, 0), 0
+    )
     replica_onehot = new_replicas[:, None] == slot_range[None, :]
     source_slot = jnp.sum(jnp.where(replica_onehot, slot_of[None, :], 0), axis=1)
     chosen_pieces = jnp.take(spread_slots, source_slot, axis=0)

time: 704 us -> 682 us (0.969)
  waiting for transfers between devices: 396 us -> 379 us
    all_to_all x1, waiting for transfers between devices: 37.6 us -> 12 us  [body(): all_to_all(jnp.stack(jnp.split(slot_weights, axis_size('req'), 2), 0), 'r...]
    unnamed x36 -> x80, local copies, waits for them, and re-layouts: 15.9 us -> 24.2 us
    all_to_all x1, waiting for transfers between devices: 145 us -> 153 us  [body(): lax.all_to_all(copies, ('req', 'exp'), split_axis=0, concat_axis=0, tiled...]
    all_to_all x2 -> x0, local copies, waits for them, and re-layouts: 8.24 us -> none  [body(): lax.all_to_all(slot_weights, 'req', split_axis=2, concat_axis=0, tiled=True)]
where the time goes in v1:
time: 682 us; the launch traced here: 671 us
  waiting for transfers between devices  379 us (56%)
  local copies, waits for them, and re-layouts  146 us (21%)
  starting transfers between devices  57.7 us (8%)
  other arithmetic  41.6 us (6%)
  matrix products  31.6 us (5%)
  between operations  15.4 us (2%)
    all_to_all x1, waiting for transfers between devices, body(): lax.all_to_all(partial_value, ('req', 'exp'), split_axis=0, concat_axis=0...  161 us
    all_to_all x1, waiting for transfers between devices, body(): lax.all_to_all(copies, ('req', 'exp'), split_axis=0, concat_axis=0, tiled...  153 us
    reduce_scatter x1, waiting for transfers between devices, body(): lax.psum_scatter(jnp.dot(attended, out_proj, preferred_element_type=jnp.f...  47.9 us
    slice x3, local copies, waits for them, and re-layouts, run_slots(): in_rows = grouped[:, slot_num].reshape(sources * capacity, model_width)  28.2 us
    unnamed x80, local copies, waits for them, and re-layouts  24.2 us
    another operation x2, local copies, waits for them, and re-layouts, run_slots(): in_rows = grouped[:, slot_num].reshape(sources * capacity, model_width)  20.1 us
    all_to_all x1, starting transfers between devices, body(): lax.all_to_all(copies, ('req', 'exp'), split_axis=0, concat_axis=0, tiled...  14.5 us
    convert_element_type x1, local copies, waits for them, and re-layouts, body(): run_slots(inbox, slot_weights, capacity).astype(jnp.bfloat16)  14 us
  transfers between devices with their start and end apart: 7, of which 5 were waited for; matrix products, arithmetic and copies ran while one was open for 26% of the time, Pallas kernels for 0%

profile of v1, /device:TPU:74, one launch (start us, length us, event | category | flops | bytes accessed | tf_op | source)
XLA Modules:
  0.0 671.4 jit_solution(14654601805482080056)
XLA Ops:
  7.2 1.1 copy.96
  9.9 8.5 %all-to-all-start = ((bf16[32,2,1,1024]{3,1,2,0:T(2,128)(2,1)}), bf16[32,2,1,1024]{3,1,2,0:T(2,128)(2,1)S(1)}, u32[]{:S(2)}, u32[]{:S(2)}) async-start(bf16[32,2,1,1024]{3,1,2,0:T(2,128)(2,1)} %maximum_bitcast_fusion), calls=%async_computation | async-start | bytes 262144 | tf_op jit(solution)/shard_map/all_to_all | solution.py:111
  23.2 1.2 fusion.52
  24.3 1.1 copy.103
  25.6 1.1 copy.105
  27.0 1.1 bitcast_dynamic-update-slice_fusion.31
  28.2 1.5 bitcast_dynamic-update-slice_fusion.30
  29.7 0.9 bitcast_dynamic-update-slice_fusion.29
  30.6 0.9 bitcast_dynamic-update-slice_fusion.28
  31.6 0.9 bitcast_dynamic-update-slice_fusion.27
  32.5 0.9 bitcast_dynamic-update-slice_fusion.26
  33.5 0.9 bitcast_dynamic-update-slice_fusion.25
  34.4 0.9 bitcast_dynamic-update-slice_fusion.24
  35.4 0.9 bitcast_dynamic-update-slice_fusion.23
  36.3 0.9 bitcast_dynamic-update-slice_fusion.22
  37.3 0.9 bitcast_dynamic-update-slice_fusion.21
  38.2 0.9 bitcast_dynamic-update-slice_fusion.20
  39.2 0.9 bitcast_dynamic-update-slice_fusion.19
  40.1 0.9 bitcast_dynamic-update-slice_fusion.18
  41.1 0.9 bitcast_dynamic-update-slice_fusion.17
  42.0 0.9 bitcast_dynamic-update-slice_fusion.16
  43.4 2.7 copy-done.3
  47.1 1.1 subtract_convert_fusion.1
  48.3 1.1 copy.94
  51.9 8.3 %all-to-all-start.1 = ((bf16[32,2,1,1024]{3,1,2,0:T(2,128)(2,1)}), bf16[32,2,1,1024]{3,1,2,0:T(2,128)(2,1)S(1)}, u32[]{:S(2)}, u32[]{:S(2)}) async-start(bf16[32,2,1,1024]{3,1,2,0:T(2,128)(2,1)} %broadcast_select_fusion.1), calls=%async_computation.1 | async-start | bytes 262144 | tf_op jit(solution)/shard_map/all_to_all | solution.py:115
  60.4 4.9 all-to-all-done.1
  65.3 8.5 %all-to-all-start.4 = ((bf16[32,2,3,64,256]{4,3,2,1,0:T(8,128)(2,1)}), bf16[32,2,3,64,256]{4,3,2,1,0:T(8,128)(2,1)}, u32[]{:S(2)}, u32[]{:S(2)}) async-start(bf16[32,2,3,64,256]{4,3,2,1,0:T(8,128)(2,1)} %copy-done.3), calls=%async_computation.5 | async-start | bytes 12582912 | tf_op jit(solution)/shard_map/all_to_all | solution.py:192
  74.1 2.7 fusion.67
  76.8 1.7 convolution_convert_fusion
  78.5 2.0 fusion.72
  80.9 1.2 reduce-window.11
  82.7 47.9 %reduce-scatter.2.cloned.1.call-done = f32[64,2048]{1,0:T(8,128)} async-done(((f32[256,2048]{1,0:T(8,128)}), f32[64,2048]{1,0:T(8,128)}) %reduce-scatter.2.cloned.1.call-update) | async-done | bytes 524304 | tf_op jit(solution)/shard_map/reduce_scatter | solution.py:142
  130.6 1.2 multiply_reduce_fusion
  131.8 1.2 multiply_convert_fusion
  133.0 5.6 scatter_custom_fusion
  138.6 5.1 broadcast_in_dim.198
  143.7 12.0 %all-to-all-done.4 = bf16[32,2,3,64,256]{4,3,2,1,0:T(8,128)(2,1)} async-done(((bf16[32,2,3,64,256]{4,3,2,1,0:T(8,128)(2,1)}), bf16[32,2,3,64,256]{4,3,2,1,0:T(8,128)(2,1)}, u32[]{:S(2)}, u32[]{:S(2)}) %all-to-all-start.4) | async-done | bytes 6291488 | tf_op jit(solution)/shard_map/all_to_all | solution.py:192
  155.7 8.1 %broadcast_in_dim.199 = bf16[32,4,20,2048]{3,2,1,0:T(8,128)(2,1)} broadcast(bf16[32,20,2048]{2,1,0:T(8,128)(2,1)} %broadcast_in_dim.198), dimensions={0,2,3} | broadcast | bytes 13107200 | tf_op jit(solution)/shard_map/broadcast_in_dim | solution.py:171
  163.8 14.5 %all-to-all-start.2 = ((bf16[128,20,2048]{2,1,0:T(8,128)(2,1)}), bf16[128,20,2048]{2,1,0:T(8,128)(2,1)}, u32[]{:S(2)}, u32[]{:S(2)}) async-start(bf16[128,20,2048]{2,1,0:T(8,128)(2,1)} %bitcast.182), calls=%async_computation.3 | async-start | bytes 25165824 | tf_op jit(solution)/shard_map/all_to_all | solution.py:175
  178.6 5.2 gather_fusion.2
  183.8 3.9 broadcast_select_fusion
  187.7 153.2 %all-to-all-done.2 = bf16[128,20,2048]{2,1,0:T(8,128)(2,1)} async-done(((bf16[128,20,2048]{2,1,0:T(8,128)(2,1)}), bf16[128,20,2048]{2,1,0:T(8,128)(2,1)}, u32[]{:S(2)}, u32[]{:S(2)}) %all-to-all-start.2) | async-done | bytes 10485792 | tf_op jit(solution)/shard_map/all_to_all | solution.py:175
  340.9 6.8 %all-to-all-start.5 = ((bf16[32,3,64,256]{3,2,1,0:T(8,128)(2,1)}), bf16[32,3,64,256]{3,2,1,0:T(8,128)(2,1)}, u32[]{:S(2)}, u32[]{:S(2)}) async-start(bf16[32,3,64,256]{3,2,1,0:T(8,128)(2,1)} %broadcast_select_fusion), calls=%async_computation.6 | async-start | bytes 6291456 | tf_op jit(solution)/shard_map/all_to_all | solution.py:197
  347.7 12.7 %copy.112 = bf16[128,20,2048]{2,0,1:T(8,128)(2,1)} copy(bf16[128,20,2048]{2,1,0:T(8,128)(2,1)} %all-to-all-done.2) | data formatting | bytes 20971520 | tf_op jit(solution)/shard_map/all_to_all | solution.py:175
  360.4 10.2 %fusion.65 = (bf16[128,1,10,2048]{3,0,2,1:T(8,128)(2,1)}, bf16[128,1,10,2048]{3,0,2,1:T(8,128)(2,1)}) fusion(bf16[128,2,10,2048]{3,0,2,1:T(8,128)(2,1)} %bitcast.183), kind=kLoop, calls=%fused_computation.166 | loop fusion | bytes 20971520 | tf_op jit(solution)/shard_map/slice | solution.py:49
  370.6 9.0 %copy.113 = bf16[128,1,10,2048]{3,2,0,1:T(8,128)(2,1)} copy(bf16[128,1,10,2048]{3,0,2,1:T(8,128)(2,1)} %get-tuple-element.13) | data formatting | bytes 10485760 | tf_op jit(solution)/shard_map/slice | solution.py:49
  379.6 10.0 %reshape_squeeze.6 = bf16[1280,2048]{1,0:T(8,128)(2,1)} reshape(bf16[128,1,10,2048]{3,2,0,1:T(8,128)(2,1)} %copy.113) | data formatting | bytes 10485760 | tf_op jit(solution)/shard_map/reshape;squeeze | solution.py:49
  389.6 4.5 fusion.17
  394.1 2.9 fusion.3
  397.3 9.0 %copy.115 = bf16[128,1,10,2048]{3,2,0,1:T(8,128)(2,1)} copy(bf16[128,1,10,2048]{3,0,2,1:T(8,128)(2,1)} %get-tuple-element.14) | data formatting | bytes 10485760 | tf_op jit(solution)/shard_map/slice | solution.py:49
  406.3 10.1 %reshape_squeeze.7 = bf16[1280,2048]{1,0:T(8,128)(2,1)} reshape(bf16[128,1,10,2048]{3,2,0,1:T(8,128)(2,1)} %copy.115) | data formatting | bytes 10485760 | tf_op jit(solution)/shard_map/reshape;squeeze | solution.py:49
  416.4 4.5 fusion.14
  420.9 3.0 fusion.4
  424.1 5.0 convert_bitcast_fusion.1
  429.1 5.2 convert_bitcast_fusion
  434.3 9.0 %pad_maximum_fusion = bf16[128,2,10,2048]{3,0,2,1:T(8,128)(2,1)} fusion(bf16[128,1,10,2048]{3,0,2,1:T(8,128)(2,1)} %convert_bitcast_fusion, bf16[128,1,10,2048]{3,0,2,1:T(8,128)(2,1)} %convert_bitcast_fusion.1), kind=kLoop, calls=%fused_computation.6 | loop fusion | flops 5242880 | bytes 20971520 | tf_op jit(solution)/shard_map/stack | solution.py:60
  443.3 14.0 %copy.117 = bf16[128,20,2048]{2,1,0:T(8,128)(2,1)} copy(bf16[128,20,2048]{2,0,1:T(8,128)(2,1)} %bitcast.184) | data formatting | bytes 20971520 | tf_op jit(solution)/shard_map/convert_element_type | solution.py:176
  457.3 11.0 %all-to-all-start.3 = ((bf16[128,20,2048]{2,1,0:T(8,128)(2,1)}), bf16[128,20,2048]{2,1,0:T(8,128)(2,1)}, u32[]{:S(2)}, u32[]{:S(2)}) async-start(bf16[128,20,2048]{2,1,0:T(8,128)(2,1)} %copy.117), calls=%async_computation.4 | async-start | bytes 25165824 | tf_op jit(solution)/shard_map/all_to_all | solution.py:177
  468.5 4.0 copy.121
  472.5 160.7 %all-to-all-done.3 = bf16[128,20,2048]{2,1,0:T(8,128)(2,1)} async-done(((bf16[128,20,2048]{2,1,0:T(8,128)(2,1)}), bf16[128,20,2048]{2,1,0:T(8,128)(2,1)}, u32[]{:S(2)}, u32[]{:S(2)}) %all-to-all-start.3) | async-done | bytes 10485792 | tf_op jit(solution)/shard_map/all_to_all | solution.py:177
  633.3 11.1 %convert_reduce_fusion = f32[32,20,2048]{2,1,0:T(8,128)} fusion(bf16[128,20,2048]{2,1,0:T(8,128)(2,1)} %all-to-all-done.3), kind=kLoop, calls=%fused_computation.5 | loop fusion | flops 9175040 | bytes 15728640 | tf_op jit(solution)/shard_map/reduce_sum | solution.py:180
  644.4 6.8 %reshape.365 = f32[640,2048]{1,0:T(8,128)} reshape(f32[32,20,2048]{2,1,0:T(8,128)} %convert_reduce_fusion) | data formatting | bytes 10485760 | tf_op jit(solution)/shard_map/reshape | solution.py:186
  651.2 8.1 %gather_fusion.1 = f32[512,2048]{1,0:T(8,128)} fusion(f32[640,2048]{1,0:T(8,128)} %reshape.365, s32[1024]{0:T(1024)S(1)} %pad_clamp_fusion.1), kind=kCustom, calls=%fused_computation.1 | custom fusion | bytes 8390656 | tf_op jit(solution)/shard_map/jit(_take)/gather | solution.py:186
  659.3 4.0 fusion.2
  (129 shorter events, 13.4 us)
Async XLA Ops:
  7.2 71.4 %copy-start = (bf16[512,2048]{1,0:T(8,128)(2,1)S(1)}, bf16[512,2048]{1,0:T(8,128)(2,1)}, u32[]{:S(2)}) copy-start(bf16[512,2048]{1,0:T(8,128)(2,1)} %param.27) | copy-start | bytes 6291460
  9.9 40.3 %all-to-all-start = ((bf16[32,2,1,1024]{3,1,2,0:T(2,128)(2,1)}), bf16[32,2,1,1024]{3,1,2,0:T(2,128)(2,1)S(1)}, u32[]{:S(2)}, u32[]{:S(2)}) async-start(bf16[32,2,1,1024]{3,1,2,0:T(2,128)(2,1)} %maximum_bitcast_fusion), calls=%async_computation | async-start | bytes 262144 | tf_op jit(solution)/shard_map/all_to_all | solution.py:111
  20.2 4.2 copy-start.11
  26.9 16.0 %copy-start.2 = (bf16[2,3,2048,256]{3,2,1,0:T(8,128)(2,1)S(1)}, bf16[2,3,2048,256]{3,2,1,0:T(8,128)(2,1)}, u32[]{:S(2)}) copy-start(bf16[2,3,2048,256]{3,2,1,0:T(8,128)(2,1)} %param.33) | copy-start | bytes 18874372
  27.0 19.0 %copy-start.14 = (pred[4]{0:T(512)(128)(4,1)S(1)}, pred[4]{0:T(512)(128)(4,1)}, u32[]{:S(2)}) copy-start(pred[4]{0:T(512)(128)(4,1)} %compare_bitcast_fusion) | copy-start | bytes 16
  27.0 19.0 %copy-start.16 = (s32[4]{0:T(128)S(1)}, s32[4]{0:T(128)}, u32[]{:S(2)}) copy-start(s32[4]{0:T(128)} %fusion.52) | copy-start | bytes 52
  27.0 19.1 %copy-start.15 = (s32[64]{0:T(128)S(1)}, s32[64]{0:T(128)}, u32[]{:S(2)}) copy-start(s32[64]{0:T(128)} %reshape.354) | copy-start | bytes 772
  27.0 19.1 %copy-start.13 = (f32[64]{0:T(128)S(1)}, f32[64]{0:T(128)}, u32[]{:S(2)}) copy-start(f32[64]{0:T(128)} %negate_power_fusion) | copy-start | bytes 772
  28.1 18.6 %copy-start.17 = (f32[128]{0:T(128)S(1)}, f32[128]{0:T(128)}, u32[]{:S(2)}) copy-start(f32[128]{0:T(128)} %param.22) | copy-start | bytes 1540
  28.1 18.6 %copy-start.18 = (f32[128]{0:T(128)S(1)}, f32[128]{0:T(128)}, u32[]{:S(2)}) copy-start(f32[128]{0:T(128)} %param.21) | copy-start | bytes 1540
  42.0 6.2 copy-start.12
  43.4 2.7 copy-start.3
  51.9 13.3 %all-to-all-start.1 = ((bf16[32,2,1,1024]{3,1,2,0:T(2,128)(2,1)}), bf16[32,2,1,1024]{3,1,2,0:T(2,128)(2,1)S(1)}, u32[]{:S(2)}, u32[]{:S(2)}) async-start(bf16[32,2,1,1024]{3,1,2,0:T(2,128)(2,1)} %broadcast_select_fusion.1), calls=%async_computation.1 | async-start | bytes 262144 | tf_op jit(solution)/shard_map/all_to_all | solution.py:115
  65.3 90.4 %all-to-all-start.4 = ((bf16[32,2,3,64,256]{4,3,2,1,0:T(8,128)(2,1)}), bf16[32,2,3,64,256]{4,3,2,1,0:T(8,128)(2,1)}, u32[]{:S(2)}, u32[]{:S(2)}) async-start(bf16[32,2,3,64,256]{4,3,2,1,0:T(8,128)(2,1)} %copy-done.3), calls=%async_computation.5 | async-start | bytes 12582912 | tf_op jit(solution)/shard_map/all_to_all | solution.py:192
  73.8 56.8 %reduce-scatter.2.cloned.1.call-start = ((), (), s32[]{:S(2)}) async-start(), calls=%async_computation.7 | async-start | bytes 2621440 | tf_op jit(solution)/shard_map/reduce_scatter | solution.py:142
  76.8 3.8 copy-start.9
  76.8 5.6 copy-start.19
  76.8 53.8 %copy-start.7 = (bf16[64,2048]{1,0:T(8,128)(2,1)S(1)}, bf16[64,2048]{1,0:T(8,128)(2,1)}, u32[]{:S(2)}) copy-start(bf16[64,2048]{1,0:T(8,128)(2,1)} %param.17) | copy-start | bytes 786436
  76.8 55.0 %copy-start.8 = (f32[2048]{0:T(1024)S(1)}, f32[2048]{0:T(1024)}, u32[]{:S(2)}) copy-start(f32[2048]{0:T(1024)} %param.28) | copy-start | bytes 24580
  163.8 14.5 %copy-start.20 = (s32[32]{0:T(128)S(1)}, s32[32]{0:T(128)}, u32[]{:S(2)}) copy-start(s32[32]{0:T(128)} %param.32) | copy-start | bytes 388
  163.8 177.0 %all-to-all-start.2 = ((bf16[128,20,2048]{2,1,0:T(8,128)(2,1)}), bf16[128,20,2048]{2,1,0:T(8,128)(2,1)}, u32[]{:S(2)}, u32[]{:S(2)}) async-start(bf16[128,20,2048]{2,1,0:T(8,128)(2,1)} %bitcast.182), calls=%async_computation.3 | async-start | bytes 25165824 | tf_op jit(solution)/shard_map/all_to_all | solution.py:175
  340.9 116.4 %all-to-all-start.5 = ((bf16[32,3,64,256]{3,2,1,0:T(8,128)(2,1)}), bf16[32,3,64,256]{3,2,1,0:T(8,128)(2,1)}, u32[]{:S(2)}, u32[]{:S(2)}) async-start(bf16[32,3,64,256]{3,2,1,0:T(8,128)(2,1)} %broadcast_select_fusion), calls=%async_computation.6 | async-start | bytes 6291456 | tf_op jit(solution)/shard_map/all_to_all | solution.py:197
  389.6 4.5 copy-start.4
  416.4 4.5 copy-start.5
  457.3 11.1 %copy-start.10 = (f32[64,8]{0,1:T(8,128)S(1)}, f32[64,8]{0,1:T(8,128)}, u32[]{:S(2)}) copy-start(f32[64,8]{0,1:T(8,128)} %param.30) | copy-start | bytes 6148
  457.3 175.9 %all-to-all-start.3 = ((bf16[128,20,2048]{2,1,0:T(8,128)(2,1)}), bf16[128,20,2048]{2,1,0:T(8,128)(2,1)}, u32[]{:S(2)}, u32[]{:S(2)}) async-start(bf16[128,20,2048]{2,1,0:T(8,128)(2,1)} %copy.117), calls=%async_computation.4 | async-start | bytes 25165824 | tf_op jit(solution)/shard_map/all_to_all | solution.py:177
  651.2 12.2 %copy-start.6 = (f32[64,2048]{1,0:T(8,128)S(1)}, f32[64,2048]{1,0:T(8,128)}, u32[]{:S(2)}) copy-start(f32[64,2048]{1,0:T(8,128)} %reduce-scatter.2.cloned.1.call-done) | copy-start | bytes 1572868
  651.2 12.9 %copy-start.1 = (bf16[512,2048]{1,0:T(8,128)(2,1)S(1)}, bf16[512,2048]{1,0:T(8,128)(2,1)}, u32[]{:S(2)}) copy-start(bf16[512,2048]{1,0:T(8,128)(2,1)} %param.27) | copy-start | bytes 6291460
Sparse Core Ops, SparseCore 0:
  80.7 49.7 reduce-scatter.1
